TPU v7x, 128 devices: a whole 4x4x4 slice. The times are simulated.
128 devices in a mesh: group: 8 (over y_hi, x), fsdp: 16 (over z, y_lo, core).
Axes of the slice: x: 4, y: 4 (y_hi: 2, y_lo: 2; y = y_hi * 2 + y_lo), z: 4, core: 2. Of those that a mesh axis runs over, the one named last changes fastest.
Arguments:
- tokens_in: bfloat16 [131072, 2048], P(('group', 'fsdp')), may hold values from -6 to 6
- out_grad: bfloat16 [131072, 2048], P(('group', 'fsdp')), may hold values from -0.59765625 to 0.59765625
- w_in: bfloat16 [8, 2048, 8192], P('group', None, 'fsdp'), may hold values from -0.125 to 0.125
- w_out: bfloat16 [8, 8192, 2048], P('group', 'fsdp'), may hold values from -0.0625 to 0.0625
- chosen: int32 [128, 8, 16], P(('group', 'fsdp')), may hold values from 0 to 1023, as said below
- counts: int32 [128, 8], P(('group', 'fsdp')), may hold values from 1 to 16, as said below
- gates: float32 [128, 8, 16], P(('group', 'fsdp')), may hold values from 0.05 to 1
Outputs:
- grad_in: bfloat16 [131072, 2048], P(('group', 'fsdp'))
- grad_w_in: float32 [8, 2048, 8192], P('group', None, 'fsdp')
- grad_w_out: float32 [8, 8192, 2048], P('group', 'fsdp')
Inputs may be any that keep to these rules, and one draw needn't show every extreme that they name: `chosen`: the 16 slots of one image and one expert name distinct positions. `counts`: each image fills all 16 slots of at least one expert.
All inputs are finite; a program needn't handle non-finite values.
Results may differ from a plain program's by a relative error of at most 0.0057.
Values may be sent and summed in bfloat16 or wider, within the bound.
A program may use at most 128 MiB of HBM per device.

v0:
```python
import jax
import jax.numpy as jnp
from jax import lax
from jax.sharding import PartitionSpec as P

gelu_coef = 0.7978845608028654


def gelu_parts(hidden):
    inner_arg = gelu_coef * (hidden + 0.044715 * hidden * hidden * hidden)
    tangent = jnp.tanh(inner_arg)
    activation = 0.5 * hidden * (1.0 + tangent)
    slope = 0.5 * (1.0 + tangent) + 0.5 * hidden * (1.0 - tangent * tangent) * gelu_coef * (
        1.0 + 3.0 * 0.044715 * hidden * hidden
    )
    return (activation, slope)


def shards(tokens_in, out_grad, w_in, w_out, chosen, counts, gates):
    group_count = lax.axis_size("group")
    exp_local = w_in.shape[0]
    slot_count = chosen.shape[2]
    model_width = tokens_in.shape[1]
    slot_rows = chosen[0].reshape(-1)
    slot_iota = lax.broadcasted_iota(jnp.int32, chosen.shape[1:], 1)
    live_gate = jnp.where(slot_iota < counts[0][:, None], gates[0], jnp.float32(0.0))
    block_shape = (group_count, exp_local, slot_count, model_width)
    picked_x = jnp.take(tokens_in, slot_rows, axis=0).reshape(block_shape)
    picked_grad = (
        (live_gate.reshape(-1)[:, None] * jnp.take(out_grad, slot_rows, axis=0).astype(jnp.float32))
        .astype(jnp.bfloat16)
        .reshape(block_shape)
    )
    near_x, near_grad = (
        lax.all_to_all(picked_x, "group", split_axis=0, concat_axis=0, tiled=True),
        lax.all_to_all(picked_grad, "group", split_axis=0, concat_axis=0, tiled=True),
    )
    rows_x, rows_grad = (
        lax.all_gather(near_x, "fsdp", axis=0, tiled=True),
        lax.all_gather(near_grad, "fsdp", axis=0, tiled=True),
    )
    sources = rows_x.shape[0]
    expert_x = rows_x[:, 0].reshape(-1, model_width)
    expert_grad = rows_grad[:, 0].reshape(-1, model_width)
    hidden = jnp.dot(expert_x, w_in[0], preferred_element_type=jnp.float32)
    activation, gelu_slope = gelu_parts(hidden)
    activation = activation.astype(jnp.bfloat16)
    back_hidden = lax.dot_general(
        expert_grad, w_out[0], (((1,), (1,)), ((), ())), preferred_element_type=jnp.float32
    )
    hidden_grad = (back_hidden * gelu_slope).astype(jnp.bfloat16)
    grads_in_w = [
        lax.dot_general(
            expert_x, hidden_grad, (((0,), (0,)), ((), ())), preferred_element_type=jnp.float32
        )
    ]
    grads_out_w = [
        lax.dot_general(
            activation, expert_grad, (((0,), (0,)), ((), ())), preferred_element_type=jnp.float32
        )
    ]
    hidden_grads = [hidden_grad.reshape(sources, slot_count, -1)]
    stacked_grad = jnp.stack(hidden_grads, axis=1)
    term = jnp.einsum("secf,edf->secd", stacked_grad, w_in, preferred_element_type=jnp.float32)
    partial_grad = term.reshape(sources * exp_local * slot_count, model_width)
    shares = lax.psum_scatter(partial_grad, "fsdp", scatter_dimension=0, tiled=True)
    summed = lax.all_to_all(
        shares.reshape(group_count, exp_local, slot_count, model_width),
        "group",
        split_axis=0,
        concat_axis=0,
        tiled=True,
    )
    grad_tokens = (
        jnp.zeros((tokens_in.shape[0], model_width), jnp.float32)
        .at[slot_rows]
        .add(summed.reshape(-1, model_width))
    )
    return (
        grad_tokens.astype(jnp.bfloat16),
        jnp.stack(grads_in_w, axis=0),
        jnp.stack(grads_out_w, axis=0),
    )


def solution(mesh):
    placed = (
        P(("group", "fsdp"), None),
        P(("group", "fsdp"), None),
        P("group", None, "fsdp"),
        P("group", "fsdp", None),
        P(("group", "fsdp"), None, None),
        P(("group", "fsdp"), None),
        P(("group", "fsdp"), None, None),
    )
    return jax.shard_map(
        shards,
        mesh=mesh,
        in_specs=placed,
        out_specs=(P(("group", "fsdp"), None), P("group", None, "fsdp"), P("group", "fsdp", None)),
        check_vma=False,
    )
```

profile of v0, /device:TPU:1, one launch (start us, length us, event | category | flops | bytes accessed | tf_op | source)
XLA Modules:
  0.0 404.0 jit_solution(8017003688771159239)
XLA Ops:
  7.2 0.0 copy-start
  7.2 0.0 copy-start.3
  7.2 0.0 copy-start.4
  7.2 0.0 all-gather.5.cloned.1.call-start
  7.2 0.9 reshape_squeeze.12
  8.2 4.2 %gather_fusion.1 = bf16[128,2048]{1,0:T(8,128)(2,1)S(1)} fusion(bf16[1024,2048]{1,0:T(8,128)(2,1)} %param.9, s32[1024]{0:T(1024)S(1)} %pad_clamp_fusion), kind=kCustom, calls=%fused_computation.1.clone | custom fusion | bytes 1049088 | tf_op jit(solution)/shard_map/jit(_take)/gather | solution.py:28
  12.4 0.1 broadcast_select_fusion
  12.5 18.1 %all_to_all.15 = bf16[8,1,16,2048]{3,2,1,0:T(8,128)(2,1)} all-to-all(bf16[8,1,16,2048]{3,2,1,0:T(8,128)(2,1)S(1)} %bitcast.43), channel_id=1, replica_groups=mesh['group'=8,'fsdp'=16] {'group'}, dimensions={0} | all-to-all | bytes 1048576 | tf_op jit(solution)/shard_map/all_to_all | solution.py:35
  30.6 0.0 all-gather.5.cloned.1.call-update
  30.6 0.0 all-gather.3.cloned.1.call-start
  30.7 0.0 copy-done.3
  30.7 0.1 squeeze.9
  30.8 0.0 copy-done.4
  30.8 0.1 iota_compare_fusion
  30.8 0.1 lt.41
  30.9 4.2 %gather_fusion = bf16[128,2048]{1,0:T(8,128)(2,1)S(1)} fusion(bf16[1024,2048]{1,0:T(8,128)(2,1)} %param.10, s32[1024]{0:T(1024)S(1)} %pad_clamp_fusion), kind=kCustom, calls=%fused_computation.clone | custom fusion | bytes 1049088 | tf_op jit(solution)/shard_map/jit(_take)/gather | solution.py:30
  35.1 0.3 multiply_convert_fusion.2
  35.4 13.5 %all_to_all.16 = bf16[8,1,16,2048]{3,2,1,0:T(8,128)(2,1)} all-to-all(bf16[8,1,16,2048]{3,2,1,0:T(8,128)(2,1)S(1)} %bitcast.42), channel_id=1, replica_groups=mesh['group'=8,'fsdp'=16] {'group'}, dimensions={0} | all-to-all | bytes 1048576 | tf_op jit(solution)/shard_map/all_to_all | solution.py:36
  49.0 0.0 all-gather.3.cloned.1.call-update
  49.0 0.0 reduce-scatter.2.cloned.1.call-start
  49.0 38.3 %all-gather.5.cloned.1.call-done = bf16[128,1,16,2048]{3,2,1,0:T(8,128)(2,1)} async-done(((bf16[8,1,16,2048]{3,2,1,0:T(8,128)(2,1)}), bf16[128,1,16,2048]{3,2,1,0:T(8,128)(2,1)}) %all-gather.5.cloned.1.call-update) | async-done | bytes 8388624 | tf_op jit(solution)/shard_map/all_gather | solution.py:39
  87.3 0.0 copy-done
  87.3 9.4 %fusion.10 = f32[2048,512]{1,0:T(8,128)} fusion(bf16[2048,2048]{1,0:T(8,128)(2,1)} %bitcast.46, bf16[1,2048,512]{2,1,0:T(8,128)(2,1)S(1)} %copy-done), kind=kOutput, calls=%fused_computation.19 | convolution fusion | flops 4294967296 | bytes 14680064 | tf_op jit(solution)/shard_map/dot_general | solution.py:45
  96.8 46.0 %all-gather.3.cloned.1.call-done = bf16[128,1,16,2048]{3,2,1,0:T(8,128)(2,1)} async-done(((bf16[8,1,16,2048]{3,2,1,0:T(8,128)(2,1)}), bf16[128,1,16,2048]{3,2,1,0:T(8,128)(2,1)}) %all-gather.3.cloned.1.call-update) | async-done | bytes 8388624 | tf_op jit(solution)/shard_map/all_gather | solution.py:40
  142.7 12.1 %fusion.6 = bf16[2048,512]{1,0:T(8,128)(2,1)S(1)} fusion(f32[2048,512]{1,0:T(8,128)} %fusion.10, bf16[2048,2048]{1,0:T(8,128)(2,1)} %bitcast.48, bf16[1,512,2048]{2,1,0:T(8,128)(2,1)} %param.12), kind=kOutput, calls=%fused_computation.12 | convolution fusion | flops 4314890240 | bytes 16777216 | tf_op jit(solution)/shard_map/dot_general | solution.py:48
  154.8 0.0 copy-start.5
  154.8 6.3 %convolution_bitcast_fusion = f32[128,1,16,2048]{3,0,2,1:T(8,128)S(1)} fusion(bf16[1,2048,512]{2,1,0:T(8,128)(2,1)S(1)} %copy-done, bf16[128,16,512]{2,1,0:T(8,128)(2,1)S(1)} %bitcast.51), kind=kOutput, calls=%fused_computation.3 | convolution fusion | flops 4294967296 | bytes 20971520 | tf_op jit(solution)/shard_map/secf,edf->secd/dot_general | solution.py:64
  161.2 0.0 copy-done.5
  161.2 19.4 %copy.16 = f32[128,1,16,2048]{3,2,0,1:T(8,128)} copy(f32[128,1,16,2048]{3,0,2,1:T(8,128)S(1)} %convolution_bitcast_fusion) | data formatting | bytes 33554432 | tf_op jit(solution)/shard_map/secf,edf->secd/transpose | solution.py:64
  180.6 0.0 copy-start.2
  180.6 0.0 reduce-scatter.2.cloned.1.call-update
  180.6 0.7 copy-done.2
  181.3 0.1 reshape_squeeze.11
  181.4 10.5 %convolution_bitcast_fusion.2 = f32[1,2048,512]{2,1,0:T(8,128)} fusion(bf16[2048,2048]{1,0:T(8,128)(2,1)} %bitcast.47, bf16[2048,512]{1,0:T(8,128)(2,1)} %copy-done.5), kind=kOutput, calls=%fused_computation.17 | convolution fusion | flops 4294967296 | bytes 14680064 | tf_op jit(solution)/shard_map/dot_general | solution.py:53
  191.9 170.1 %reduce-scatter.2.cloned.1.call-done = f32[128,2048]{1,0:T(8,128)} async-done(((f32[2048,2048]{1,0:T(8,128)}), f32[128,2048]{1,0:T(8,128)}) %reduce-scatter.2.cloned.1.call-update) | async-done | bytes 1048592 | tf_op jit(solution)/shard_map/reduce_scatter | solution.py:66
  362.0 6.1 %all-to-all-start.2 = ((f32[8,1,16,2048]{3,2,1,0:T(8,128)}), f32[8,1,16,2048]{3,2,1,0:T(8,128)S(1)}, u32[]{:S(2)}, u32[]{:S(2)}) async-start(f32[8,1,16,2048]{3,2,1,0:T(8,128)} %bitcast.44), calls=%async_computation.3 | async-start | bytes 2097152 | tf_op jit(solution)/shard_map/all_to_all | solution.py:67
  368.2 11.5 %convolution_bitcast_fusion.1 = f32[1,512,2048]{2,1,0:T(8,128)} fusion(bf16[2048,2048]{1,0:T(8,128)(2,1)} %bitcast.49, f32[2048,512]{1,0:T(8,128)} %fusion.10), kind=kOutput, calls=%fused_computation.16 | convolution fusion | flops 4304404480 | bytes 16777216 | tf_op jit(solution)/shard_map/dot_general | solution.py:58
  379.7 5.8 %all-to-all-done.2 = f32[8,1,16,2048]{3,2,1,0:T(8,128)S(1)} async-done(((f32[8,1,16,2048]{3,2,1,0:T(8,128)}), f32[8,1,16,2048]{3,2,1,0:T(8,128)S(1)}, u32[]{:S(2)}, u32[]{:S(2)}) %all-to-all-start.2) | async-done | bytes 1048608 | tf_op jit(solution)/shard_map/all_to_all | solution.py:67
  385.6 0.0 copy-start.1
  385.6 5.8 %scatter_custom_fusion = f32[1024,2048]{1,0:T(8,128)} fusion(s32[128]{0:T(128)S(1)} %fusion.18, f32[128,2048]{1,0:T(8,128)S(1)} %bitcast.45, f32[]{:T(128)} %constant.0.clone.1), kind=kCustom, calls=%fused_computation.14 | custom fusion | flops 262144 | bytes 8388612 | tf_op jit(solution)/shard_map/scatter-add | solution.py:77
  391.4 6.0 %convert_element_type.18 = bf16[1024,2048]{1,0:T(8,128)(2,1)} convert(f32[1024,2048]{1,0:T(8,128)} %scatter_custom_fusion) | non-fusion elementwise | flops 2097152 | bytes 12582912 | tf_op jit(solution)/shard_map/convert_element_type | solution.py:80
  397.4 0.0 copy-done.1
  (5 shorter events, 0.0 us)
Async XLA Ops:
  7.2 80.2 %copy-start = (bf16[1,2048,512]{2,1,0:T(8,128)(2,1)S(1)}, bf16[1,2048,512]{2,1,0:T(8,128)(2,1)}, u32[]{:S(2)}) copy-start(bf16[1,2048,512]{2,1,0:T(8,128)(2,1)} %param.11) | copy-start | bytes 6291460
  7.2 23.5 %copy-start.3 = (f32[1,8,16]{2,1,0:T(8,128)S(1)}, f32[1,8,16]{2,1,0:T(8,128)}, u32[]{:S(2)}) copy-start(f32[1,8,16]{2,1,0:T(8,128)} %param.15) | copy-start | bytes 1540
  7.2 23.6 %copy-start.4 = (s32[1,8]{1,0:T(1,128)S(1)}, s32[1,8]{1,0:T(1,128)}, u32[]{:S(2)}) copy-start(s32[1,8]{1,0:T(1,128)} %param.14) | copy-start | bytes 100
  7.2 80.1 %all-gather.5.cloned.1.call-start = ((), (), s32[]{:S(2)}) async-start(), calls=%async_computation.5 | async-start | bytes 8912896 | tf_op jit(solution)/shard_map/all_gather | solution.py:39
  30.6 112.1 %all-gather.3.cloned.1.call-start = ((), (), s32[]{:S(2)}) async-start(), calls=%async_computation.4 | async-start | bytes 8912896 | tf_op jit(solution)/shard_map/all_gather | solution.py:40
  49.0 313.1 %reduce-scatter.2.cloned.1.call-start = ((), (), s32[]{:S(2)}) async-start(), calls=%async_computation.6 | async-start | bytes 17825792 | tf_op jit(solution)/shard_map/reduce_scatter | solution.py:66
  154.8 6.3 %copy-start.5 = (bf16[2048,512]{1,0:T(8,128)(2,1)}, bf16[2048,512]{1,0:T(8,128)(2,1)S(1)}, u32[]{:S(2)}) copy-start(bf16[2048,512]{1,0:T(8,128)(2,1)S(1)} %fusion.6) | copy-start | bytes 6291460
  180.6 0.7 copy-start.2
  362.0 23.5 %all-to-all-start.2 = ((f32[8,1,16,2048]{3,2,1,0:T(8,128)}), f32[8,1,16,2048]{3,2,1,0:T(8,128)S(1)}, u32[]{:S(2)}, u32[]{:S(2)}) async-start(f32[8,1,16,2048]{3,2,1,0:T(8,128)} %bitcast.44), calls=%async_computation.3 | async-start | bytes 2097152 | tf_op jit(solution)/shard_map/all_to_all | solution.py:67
  385.6 11.9 %copy-start.1 = (bf16[1,2048,512]{2,1,0:T(8,128)(2,1)S(1)}, bf16[1,2048,512]{2,1,0:T(8,128)(2,1)}, u32[]{:S(2)}) copy-start(bf16[1,2048,512]{2,1,0:T(8,128)(2,1)} %param.11) | copy-start | bytes 6291460
Sparse Core Ops, SparseCore 0:
  30.7 56.5 all-gather.4
  89.0 53.6 all-gather.2
  180.7 181.2 reduce-scatter.1
where the time goes:
time: 404 us
  waiting for transfers between devices  260 us (64%)
  matrix products  49.9 us (12%)
  blocking collectives  31.6 us (8%)
  local copies, waits for them, and re-layouts  29.6 us (7%)
  between operations  13.9 us (3%)
  other arithmetic  12.4 us (3%)
  starting transfers between devices  6.26 us (2%)
    reduce_scatter x1, waiting for transfers between devices, shards(): lax.psum_scatter(partial_grad, 'fsdp', scatter_dimension=0, tiled=True)  170 us
    all_gather x1, waiting for transfers between devices, shards(): lax.all_gather(near_grad, 'fsdp', axis=0, tiled=True)  46 us
    all_gather x1, waiting for transfers between devices, shards(): lax.all_gather(near_x, 'fsdp', axis=0, tiled=True)  38.3 us
    transpose x1, local copies, waits for them, and re-layouts, shards(): jnp.einsum('secf,edf->secd', stacked_grad, w_in, preferred_element_type=j...  19.4 us
    all_to_all x1, blocking collectives, shards(): lax.all_to_all(picked_x, 'group', split_axis=0, concat_axis=0, tiled=True)  18.1 us
    all_to_all x1, blocking collectives, shards(): lax.all_to_all(picked_grad, 'group', split_axis=0, concat_axis=0, tiled=T...  13.5 us
    dot_general x1, matrix products, shards(): lax.dot_general(expert_grad, w_out[0], (((1,), (1,)), ((), ())), preferre...  12.1 us
    dot_general x1, matrix products, shards(): lax.dot_general(activation, expert_grad, (((0,), (0,)), ((), ())), prefer...  11.5 us
  transfers between devices with their start and end apart: 4, of which 4 were waited for; matrix products, arithmetic and copies ran while one was open for 9% of the time, Pallas kernels for 0%

commit v1 on v0

--- a/solution.py
+++ b/solution.py
@@ -36,7 +36,9 @@
         lax.all_to_all(picked_grad, "group", split_axis=0, concat_axis=0, tiled=True),
     )
     rows_x, rows_grad = (
-        lax.all_gather(near_x, "fsdp", axis=0, tiled=True),
+        jnp.concatenate(
+            lax.all_to_all(jnp.stack([near_x] * lax.axis_size("fsdp")), "fsdp", 0, 0), axis=0
+        ),
         lax.all_gather(near_grad, "fsdp", axis=0, tiled=True),
     )
     sources = rows_x.shape[0]

time: 404 us -> 450 us (1.11)
  blocking collectives: 31.6 us -> 161 us
  waiting for transfers between devices: 260 us -> 174 us
  local copies, waits for them, and re-layouts: 29.6 us -> 34.6 us
    all_to_all x0 -> x1, blocking collectives: none -> 130 us  [shards(): lax.all_to_all(jnp.stack([near_x] * lax.axis_size('fsdp')), 'fsdp', 0, 0)]
    all_gather x1, waiting for transfers between devices: 46 us -> 0.01 us  [shards(): lax.all_gather(near_grad, 'fsdp', axis=0, tiled=True)]
    all_gather x1 -> x0, waiting for transfers between devices: 38.3 us -> none  [shards(): lax.all_gather(near_x, 'fsdp', axis=0, tiled=True)]
    all_to_all x1, blocking collectives: 18.1 us -> 12.9 us  [shards(): lax.all_to_all(picked_x, 'group', split_axis=0, concat_axis=0, tiled=True)]
    all_to_all x1, blocking collectives: 13.5 us -> 18.1 us  [shards(): lax.all_to_all(picked_grad, 'group', split_axis=0, concat_axis=0, tiled=T...]
  transfers between devices with their start and end apart: 4 -> 3, of which waited for: 4 -> 2; matrix products, arithmetic and copies ran while one was open for 9% -> 7% of each run, Pallas kernels for 0% -> 0%
where the time goes in v1:
time: 450 us
  waiting for transfers between devices  174 us (39%)
  blocking collectives  161 us (36%)
  matrix products  46.4 us (10%)
  local copies, waits for them, and re-layouts  34.6 us (8%)
  between operations  14.1 us (3%)
  other arithmetic  13.1 us (3%)
  starting transfers between devices  6.22 us (1%)
    reduce_scatter x1, waiting for transfers between devices, shards(): lax.psum_scatter(partial_grad, 'fsdp', scatter_dimension=0, tiled=True)  169 us
    all_to_all x1, blocking collectives, shards(): lax.all_to_all(jnp.stack([near_x] * lax.axis_size('fsdp')), 'fsdp', 0, 0)  130 us
    transpose x1, local copies, waits for them, and re-layouts, shards(): jnp.einsum('secf,edf->secd', stacked_grad, w_in, preferred_element_type=j...  19.4 us
    all_to_all x1, blocking collectives, shards(): lax.all_to_all(picked_grad, 'group', split_axis=0, concat_axis=0, tiled=T...  18.1 us
    all_to_all x1, blocking collectives, shards(): lax.all_to_all(picked_x, 'group', split_axis=0, concat_axis=0, tiled=True)  12.9 us
    dot_general x1, matrix products, shards(): lax.dot_general(expert_grad, w_out[0], (((1,), (1,)), ((), ())), preferre...  12.1 us
    dot_general x1, matrix products, shards(): lax.dot_general(activation, expert_grad, (((0,), (0,)), ((), ())), prefer...  11.5 us
    dot_general x1, matrix products, shards(): lax.dot_general(expert_x, hidden_grad, (((0,), (0,)), ((), ())), preferre...  10.6 us
  transfers between devices with their start and end apart: 3, of which 2 were waited for; matrix products, arithmetic and copies ran while one was open for 7% of the time, Pallas kernels for 0%

profile of v1, /device:TPU:1, one launch (start us, length us, event | category | flops | bytes accessed | tf_op | source)
XLA Modules:
  0.0 449.5 jit_solution(3019836448391505547)
XLA Ops:
  7.2 0.0 copy-start
  7.2 0.0 all-gather.2.cloned.1.call-start
  7.2 0.9 reshape_squeeze.9
  8.2 0.8 squeeze.9
  8.9 0.7 iota_compare_fusion
  9.7 0.1 lt.41
  9.8 4.2 gather_fusion
  13.9 0.3 multiply_convert_fusion.2
  14.2 18.1 %all_to_all.23 = bf16[8,1,16,2048]{3,2,1,0:T(8,128)(2,1)} all-to-all(bf16[8,1,16,2048]{3,2,1,0:T(8,128)(2,1)S(1)} %bitcast.46), channel_id=1, replica_groups=mesh['group'=8,'fsdp'=16] {'group'}, dimensions={0} | all-to-all | bytes 1048576 | tf_op jit(solution)/shard_map/all_to_all | solution.py:36
  32.3 0.0 all-gather.2.cloned.1.call-update
  32.4 0.0 reduce-scatter.2.cloned.1.call-start
  32.4 4.2 gather_fusion.1
  36.6 0.1 broadcast_select_fusion
  36.7 12.9 %all_to_all.24 = bf16[8,1,16,2048]{3,2,1,0:T(8,128)(2,1)S(1)} all-to-all(bf16[8,1,16,2048]{3,2,1,0:T(8,128)(2,1)S(1)} %bitcast.47), channel_id=1, replica_groups=mesh['group'=8,'fsdp'=16] {'group'}, dimensions={0} | all-to-all | bytes 1048576 | tf_op jit(solution)/shard_map/all_to_all | solution.py:35
  49.6 1.1 stack.6
  50.7 129.6 %all_to_all.25 = bf16[16,8,1,16,2048]{4,3,2,1,0:T(8,128)(2,1)S(1)} all-to-all(bf16[16,8,1,16,2048]{4,3,2,1,0:T(8,128)(2,1)S(1)} %stack.6), channel_id=1, replica_groups=mesh['group'=8,'fsdp'=16] {'fsdp'}, dimensions={0} | all-to-all | bytes 16777216 | tf_op jit(solution)/shard_map/all_to_all | solution.py:40
  180.3 0.0 copy-start.2
  180.3 3.2 copy-done.2
  183.5 0.0 copy-done
  183.5 6.0 %fusion.10 = f32[2048,512]{1,0:T(8,128)} fusion(bf16[2048,2048]{1,0:T(8,128)(2,1)S(1)} %bitcast.43, bf16[1,2048,512]{2,1,0:T(8,128)(2,1)S(1)} %copy-done), kind=kOutput, calls=%fused_computation.19 | convolution fusion | flops 4294967296 | bytes 14680064 | tf_op jit(solution)/shard_map/dot_general | solution.py:47
  189.5 0.0 all-gather.2.cloned.1.call-done
  189.5 12.1 %fusion.6 = bf16[2048,512]{1,0:T(8,128)(2,1)S(1)} fusion(f32[2048,512]{1,0:T(8,128)} %fusion.10, bf16[2048,2048]{1,0:T(8,128)(2,1)} %bitcast.50, bf16[1,512,2048]{2,1,0:T(8,128)(2,1)} %param.12), kind=kOutput, calls=%fused_computation.12 | convolution fusion | flops 4314890240 | bytes 16777216 | tf_op jit(solution)/shard_map/dot_general | solution.py:50
  201.6 0.0 copy-start.4
  201.6 6.3 %convolution_bitcast_fusion = f32[128,1,16,2048]{3,0,2,1:T(8,128)S(1)} fusion(bf16[1,2048,512]{2,1,0:T(8,128)(2,1)S(1)} %copy-done, bf16[128,16,512]{2,1,0:T(8,128)(2,1)S(1)} %bitcast.53), kind=kOutput, calls=%fused_computation.3 | convolution fusion | flops 4294967296 | bytes 20971520 | tf_op jit(solution)/shard_map/secf,edf->secd/dot_general | solution.py:66
  207.9 0.0 copy-done.4
  207.9 19.4 %copy.16 = f32[128,1,16,2048]{3,2,0,1:T(8,128)} copy(f32[128,1,16,2048]{3,0,2,1:T(8,128)S(1)} %convolution_bitcast_fusion) | data formatting | bytes 33554432 | tf_op jit(solution)/shard_map/secf,edf->secd/transpose | solution.py:66
  227.3 0.0 copy-start.3
  227.3 0.0 reduce-scatter.2.cloned.1.call-update
  227.4 0.7 copy-done.3
  228.0 0.1 reshape_squeeze.8
  228.1 10.6 %convolution_bitcast_fusion.2 = f32[1,2048,512]{2,1,0:T(8,128)} fusion(bf16[2048,2048]{1,0:T(8,128)(2,1)} %bitcast.44, bf16[2048,512]{1,0:T(8,128)(2,1)} %copy-done.4), kind=kOutput, calls=%fused_computation.17 | convolution fusion | flops 4294967296 | bytes 14680064 | tf_op jit(solution)/shard_map/dot_general | solution.py:55
  238.7 168.6 %reduce-scatter.2.cloned.1.call-done = f32[128,2048]{1,0:T(8,128)} async-done(((f32[2048,2048]{1,0:T(8,128)}), f32[128,2048]{1,0:T(8,128)}) %reduce-scatter.2.cloned.1.call-update) | async-done | bytes 1048592 | tf_op jit(solution)/shard_map/reduce_scatter | solution.py:68
  407.2 6.1 %all-to-all-start.3 = ((f32[8,1,16,2048]{3,2,1,0:T(8,128)}), f32[8,1,16,2048]{3,2,1,0:T(8,128)S(1)}, u32[]{:S(2)}, u32[]{:S(2)}) async-start(f32[8,1,16,2048]{3,2,1,0:T(8,128)} %bitcast.48), calls=%async_computation.4 | async-start | bytes 2097152 | tf_op jit(solution)/shard_map/all_to_all | solution.py:69
  413.4 11.5 %convolution_bitcast_fusion.1 = f32[1,512,2048]{2,1,0:T(8,128)} fusion(bf16[2048,2048]{1,0:T(8,128)(2,1)} %bitcast.51, f32[2048,512]{1,0:T(8,128)} %fusion.10), kind=kOutput, calls=%fused_computation.16 | convolution fusion | flops 4304404480 | bytes 16777216 | tf_op jit(solution)/shard_map/dot_general | solution.py:60
  424.9 5.8 %all-to-all-done.3 = f32[8,1,16,2048]{3,2,1,0:T(8,128)S(1)} async-done(((f32[8,1,16,2048]{3,2,1,0:T(8,128)}), f32[8,1,16,2048]{3,2,1,0:T(8,128)S(1)}, u32[]{:S(2)}, u32[]{:S(2)}) %all-to-all-start.3) | async-done | bytes 1048608 | tf_op jit(solution)/shard_map/all_to_all | solution.py:69
  430.7 0.0 copy-start.1
  430.8 5.9 %scatter_custom_fusion = f32[1024,2048]{1,0:T(8,128)} fusion(s32[128]{0:T(128)S(1)} %fusion.18, f32[128,2048]{1,0:T(8,128)S(1)} %bitcast.49, f32[]{:T(128)} %constant.0.clone.1), kind=kCustom, calls=%fused_computation.14 | custom fusion | flops 262144 | bytes 8388612 | tf_op jit(solution)/shard_map/scatter-add | solution.py:79
  436.6 6.0 %convert_element_type.18 = bf16[1024,2048]{1,0:T(8,128)(2,1)} convert(f32[1024,2048]{1,0:T(8,128)} %scatter_custom_fusion) | non-fusion elementwise | flops 2097152 | bytes 12582912 | tf_op jit(solution)/shard_map/convert_element_type | solution.py:82
  442.7 0.0 copy-done.1
  (5 shorter events, 0.0 us)
Async XLA Ops:
  7.2 176.3 %copy-start = (bf16[1,2048,512]{2,1,0:T(8,128)(2,1)S(1)}, bf16[1,2048,512]{2,1,0:T(8,128)(2,1)}, u32[]{:S(2)}) copy-start(bf16[1,2048,512]{2,1,0:T(8,128)(2,1)} %param.11) | copy-start | bytes 6291460
  7.2 182.3 %all-gather.2.cloned.1.call-start = ((), (), s32[]{:S(2)}) async-start(), calls=%async_computation.5 | async-start | bytes 8912896 | tf_op jit(solution)/shard_map/all_gather | solution.py:42
  32.4 374.9 %reduce-scatter.2.cloned.1.call-start = ((), (), s32[]{:S(2)}) async-start(), calls=%async_computation.6 | async-start | bytes 17825792 | tf_op jit(solution)/shard_map/reduce_scatter | solution.py:68
  180.3 3.2 copy-start.2
  201.6 6.3 %copy-start.4 = (bf16[2048,512]{1,0:T(8,128)(2,1)}, bf16[2048,512]{1,0:T(8,128)(2,1)S(1)}, u32[]{:S(2)}) copy-start(bf16[2048,512]{1,0:T(8,128)(2,1)S(1)} %fusion.6) | copy-start | bytes 6291460
  227.3 0.7 copy-start.3
  407.2 23.5 %all-to-all-start.3 = ((f32[8,1,16,2048]{3,2,1,0:T(8,128)}), f32[8,1,16,2048]{3,2,1,0:T(8,128)S(1)}, u32[]{:S(2)}, u32[]{:S(2)}) async-start(f32[8,1,16,2048]{3,2,1,0:T(8,128)} %bitcast.48), calls=%async_computation.4 | async-start | bytes 2097152 | tf_op jit(solution)/shard_map/all_to_all | solution.py:69
  430.7 11.9 %copy-start.1 = (bf16[1,2048,512]{2,1,0:T(8,128)(2,1)S(1)}, bf16[1,2048,512]{2,1,0:T(8,128)(2,1)}, u32[]{:S(2)}) copy-start(bf16[1,2048,512]{2,1,0:T(8,128)(2,1)} %param.11) | copy-start | bytes 6291460
Sparse Core Ops, SparseCore 0:
  32.5 129.9 all-gather.1
  227.5 179.7 reduce-scatter.1
